TPU v7x, 512 devices: a whole 4x8x8 slice. The times are simulated.
512 devices in a mesh: tp: 8 (over x, y_hi), seq: 64 (over z, y_lo, core).
Axes of the slice: x: 4, y: 8 (y_hi: 2, y_lo: 4; y = y_hi * 4 + y_lo), z: 8, core: 2. Of those that a mesh axis runs over, the one named last changes fastest.
Arguments:
- llama_context: bfloat16 [512, 4096], P(None, 'tp'), may hold values from -6 to 6
- llama_residual: bfloat16 [512, 4096], P(None, 'seq'), may hold values from -6 to 6
- w_attn_out: bfloat16 [4096, 4096], P('tp', 'seq'), may hold values from -0.09375 to 0.09375
- w_caption: bfloat16 [4096, 2560], P('seq', 'tp'), may hold values from -0.09375 to 0.09375
- w_text_kv: bfloat16 [2560, 2, 2048], P(None, None, 'tp'), may hold values from -0.125 to 0.125
- prompt_length: int32 [4], replicated, may hold values from 1 to 128, as said below
- image_query: bfloat16 [2, 16384, 2048], P(None, 'seq', 'tp'), may hold values from -32 to 32
- image_key: bfloat16 [2, 16384, 2048], P(None, 'seq', 'tp'), may hold values from -9 to 9
- image_value: bfloat16 [2, 16384, 2048], P(None, 'seq', 'tp'), may hold values from -6 to 6
Outputs:
- joint_context: bfloat16 [2, 16384, 2048], P(None, 'seq', 'tp')
Inputs may be any that keep to these rules, and one draw needn't show every extreme that they name: `prompt_length`: one pair's prompt has all 128 tokens live, every other pair's fewer.
All inputs are finite; a program needn't handle non-finite values.
Results may differ from a plain program's by a relative error of at most 0.039.
Values may be sent and summed in bfloat16 or wider, within the bound.
No kernel may reach another device: no remote copies, remote signals or barrier semaphores. Data moves between devices by JAX's collectives and lax.ppermute only.
A program may use at most 64 MiB of HBM per device.

v0:
```python
import math
import jax
import jax.numpy as jnp
from jax import lax
from jax.sharding import PartitionSpec as P

TXT = 128
HD = 128
IMG = 4096


def partner(value, axis, apart):
    mask = 2**apart
    pairs = [(source, source ^ mask) for source in range(lax.axis_size(axis))]
    return lax.ppermute(value, axis, pairs)


def local(
    llama_context,
    llama_residual,
    w_attn_out,
    w_caption,
    w_text_kv,
    prompt_length,
    image_query,
    image_key,
    image_value,
):
    llama_term = jnp.dot(llama_context, w_attn_out, preferred_element_type=jnp.float32)
    llama_attn = lax.psum(llama_term.astype(jnp.bfloat16), "tp").astype(jnp.float32)
    llama_hidden = (llama_residual.astype(jnp.float32) + llama_attn).astype(jnp.bfloat16)
    seq_index = lax.axis_index("seq")
    side_count, row_count, local_width = image_query.shape
    group_size = IMG // row_count
    text_rows = TXT // group_size
    caption_term = jnp.dot(llama_hidden, w_caption, preferred_element_type=jnp.float32)
    caption_whole = lax.psum(caption_term, "seq")
    text_part = lax.dynamic_slice_in_dim(caption_whole, seq_index * text_rows, text_rows, 0)
    text_states = lax.all_gather(text_part.astype(jnp.bfloat16), "tp", axis=1, tiled=True)
    text_kv = jnp.einsum(
        "td,djc->tjc", text_states, w_text_kv, preferred_element_type=jnp.float32
    ).astype(jnp.bfloat16)
    member = seq_index % group_size
    pair_index = seq_index // group_size
    pair_count = prompt_length.shape[0]
    live_length = jnp.sum(
        jnp.where(jnp.arange(pair_count, dtype=jnp.int32) == pair_index, prompt_length, 0)
    )
    text_place = member * text_rows + jnp.arange(text_rows, dtype=jnp.int32)
    text_bias = jnp.where(text_place < live_length, 0.0, -1e30).astype(jnp.bfloat16)
    local_heads = local_width // HD
    scale_factor = 1.0 / math.sqrt(HD)
    queries = image_query.reshape(side_count, row_count, local_heads, HD)

    def absorb(running, pieces):
        old_max, old_totals, old_accum = running
        text_piece, bias_piece, key_piece, value_piece = pieces
        text_count = text_piece.shape[0]
        piece_rows = key_piece.shape[1]
        text_keys = text_piece[:, 0].reshape(text_count, local_heads, HD)
        text_values = text_piece[:, 1].reshape(text_count, local_heads, HD)
        key_heads = key_piece.reshape(side_count, piece_rows, local_heads, HD)
        value_heads = value_piece.reshape(side_count, piece_rows, local_heads, HD)
        text_scores = (
            jnp.einsum("srhd,thd->shrt", queries, text_keys, preferred_element_type=jnp.float32)
            * scale_factor
        )
        text_scores = text_scores + bias_piece.astype(jnp.float32)[None, None, None, :]
        image_scores = (
            jnp.einsum("srhd,snhd->shrn", queries, key_heads, preferred_element_type=jnp.float32)
            * scale_factor
        )
        new_max = jnp.maximum(
            old_max, jnp.maximum(jnp.max(text_scores, axis=-1), jnp.max(image_scores, axis=-1))
        )
        factor = jnp.exp(old_max - new_max)
        text_weights = jnp.exp(text_scores - new_max[..., None])
        image_weights = jnp.exp(image_scores - new_max[..., None])
        new_totals = (
            old_totals * factor + jnp.sum(text_weights, axis=-1) + jnp.sum(image_weights, axis=-1)
        )
        addition = jnp.einsum(
            "shrt,thd->shrd",
            text_weights.astype(jnp.bfloat16),
            text_values,
            preferred_element_type=jnp.float32,
        )
        addition = addition + jnp.einsum(
            "shrn,snhd->shrd",
            image_weights.astype(jnp.bfloat16),
            value_heads,
            preferred_element_type=jnp.float32,
        )
        return (new_max, new_totals, old_accum * factor[..., None] + addition)

    start_max = jnp.full((side_count, local_heads, row_count), -1e30, jnp.float32)
    start_totals = jnp.zeros((side_count, local_heads, row_count), jnp.float32)
    start_accum = jnp.zeros((side_count, local_heads, row_count, HD), jnp.float32)
    collected = (text_kv, text_bias, image_key, image_value)
    running = absorb((start_max, start_totals, start_accum), collected)
    levels = group_size.bit_length() - 1
    bit_order = list(range(levels))
    for position, bit_number in enumerate(bit_order):
        arrived = partner(
            (collected[0], collected[1], collected[2], collected[3]), "seq", bit_number
        )
        running = absorb(running, arrived)
        if position + 1 < levels:
            collected = (
                jnp.concatenate((collected[0], arrived[0]), axis=0),
                jnp.concatenate((collected[1], arrived[1]), axis=0),
                jnp.concatenate((collected[2], arrived[2]), axis=1),
                jnp.concatenate((collected[3], arrived[3]), axis=1),
            )
    final_max, final_totals, final_accum = running
    context = (final_accum / final_totals[..., None]).astype(jnp.bfloat16)
    return context.transpose(0, 2, 1, 3).reshape(side_count, row_count, local_width)


def solution(mesh):
    placed = (
        P(None, "tp"),
        P(None, "seq"),
        P("tp", "seq"),
        P("seq", "tp"),
        P(None, None, "tp"),
        P(),
        P(None, "seq", "tp"),
        P(None, "seq", "tp"),
        P(None, "seq", "tp"),
    )
    return jax.shard_map(
        local, mesh=mesh, in_specs=placed, out_specs=P(None, "seq", "tp"), check_vma=False
    )
```

profile of v0, /device:TPU:1, one launch (start us, length us, event | category | flops | bytes accessed | tf_op | source)
XLA Modules:
  0.0 641.8 jit_solution(18367367319555831022)
XLA Ops:
  6.6 1.4 fusion.127
  9.2 8.7 %collective-permute-start.1 = (bf16[8]{0:T(256)(128)(2,1)S(1)}, bf16[8]{0:T(256)(128)(2,1)S(1)}, u32[]{:S(2)}, u32[]{:S(2)}) collective-permute-start(bf16[8]{0:T(256)(128)(2,1)S(1)} %get-tuple-element.18), channel_id=1, source_target_pairs={{0,1},{1,0},{2,3},{3,2},{4,5},{5,4},{6,7},{7,6},{8,9},{9,8},{10,11... | collective-permute-start | bytes 56 | tf_op jit(solution)/shard_map/ppermute | solution.py:15
  17.9 2.0 convolution_convert_fusion
  21.0 1.9 collective-permute-start.2
  22.9 1.8 copy.212
  24.7 2.4 collective-permute-start.3
  27.1 2.9 fusion.150
  30.1 1.9 collective-permute-start.5
  32.0 2.4 collective-permute-done.5
  34.5 1.9 collective-permute-start.9
  36.9 2.7 collective-permute-done.9
  39.7 1.9 collective-permute-start.13
  44.6 79.9 %all-reduce.3.cloned.1.call-done = bf16[512,64]{0,1:T(8,128)(2,1)} async-done(((bf16[512,64]{0,1:T(8,128)(2,1)}), bf16[512,64]{0,1:T(8,128)(2,1)}) %all-reduce.3.cloned.1.call-update) | async-done | bytes 65552 | tf_op jit(solution)/shard_map/psum | solution.py:30
  124.6 2.0 fusion.97
  126.6 272.4 %all-reduce.4 = bf16[512,320]{1,0:T(8,128)(2,1)} all-reduce(f32[512,320]{1,0:T(8,128)} %fusion.97), channel_id=1, replica_groups=mesh['tp'=8,'seq'=64] {'seq'}, use_global_device_ids=true, to_apply=%region_1.0 | all-reduce | flops 163840 | bytes 983040 | tf_op jit(solution)/shard_map/psum | solution.py:37
  399.6 37.7 %all-gather = bf16[8,320,8]{1,2,0:T(8,128)(2,1)S(1)} all-gather(bf16[1,320,8]{1,2,0:T(8,128)(2,1)S(1)} %fusion.117), channel_id=1, replica_groups=mesh['tp'=8,'seq'=64] {'tp'}, dimensions={0}, use_global_device_ids=true | all-gather | bytes 46080 | tf_op jit(solution)/shard_map/all_gather | solution.py:39
  437.9 14.5 %collective-permute-start = (bf16[8,2,256]{2,0,1:T(8,128)(2,1)S(1)}, bf16[8,2,256]{2,0,1:T(8,128)(2,1)S(1)}, u32[]{:S(2)}, u32[]{:S(2)}) collective-permute-start(bf16[8,2,256]{2,0,1:T(8,128)(2,1)S(1)} %fusion.50), channel_id=1, source_target_pairs={{0,1},{1,0},{2,3},{3,2},{4,5},{5,4},{6,7},{7,6},{8,9},{9,8},{10,11... | collective-permute-start | bytes 24584 | tf_op jit(solution)/shard_map/ppermute | solution.py:15
  453.2 1.9 collective-permute-start.4
  456.7 3.3 collective-permute-start.6
  461.5 1.9 collective-permute-start.8
  464.6 8.0 %collective-permute-done.6 = bf16[2,512,256]{1,2,0:T(8,128)(2,1)S(1)} collective-permute-done((bf16[2,512,256]{1,2,0:T(8,128)(2,1)}, bf16[2,512,256]{1,2,0:T(8,128)(2,1)S(1)}, u32[]{:S(2)}, u32[]{:S(2)}) %collective-permute-start.6) | collective-permute-done | bytes 524320 | tf_op jit(solution)/shard_map/ppermute | solution.py:15
  472.6 2.2 pad_maximum_fusion.2
  474.8 1.9 collective-permute-start.10
  476.7 1.4 fusion.146
  479.5 1.4 pad_maximum_fusion.6
  480.9 1.9 collective-permute-start.12
  482.8 1.3 fusion.142
  485.4 1.3 reshape_squeeze.37
  486.8 2.2 fusion.145
  488.9 1.9 pad_maximum_fusion.5
  490.8 2.4 collective-permute-start.7
  493.2 1.4 fusion.141
  494.6 1.4 reshape_squeeze.38
  496.0 29.3 %collective-permute-done.10 = bf16[2,1024,256]{1,2,0:T(8,128)(2,1)} collective-permute-done((bf16[2,1024,256]{1,2,0:T(8,128)(2,1)}, bf16[2,1024,256]{1,2,0:T(8,128)(2,1)}, u32[]{:S(2)}, u32[]{:S(2)}) %collective-permute-start.10) | collective-permute-done | bytes 1048608 | tf_op jit(solution)/shard_map/ppermute | solution.py:15
  525.3 3.0 pad_maximum_fusion
  528.3 1.9 collective-permute-start.14
  530.2 1.5 fusion.144
  531.7 1.4 reshape_squeeze.39
  533.1 1.3 pad_maximum_fusion.3
  534.5 1.9 collective-permute-start.11
  538.1 44.0 %collective-permute-done.11 = bf16[2,1024,256]{1,2,0:T(8,128)(2,1)S(1)} collective-permute-done((bf16[2,1024,256]{1,2,0:T(8,128)(2,1)S(1)}, bf16[2,1024,256]{1,2,0:T(8,128)(2,1)S(1)}, u32[]{:S(2)}, u32[]{:S(2)}) %collective-permute-start.11) | collective-permute-done | bytes 1048608 | tf_op jit(solution)/shard_map/ppermute | solution.py:15
  582.1 1.4 pad_maximum_fusion.1
  583.5 3.5 collective-permute-start.15
  587.1 2.0 bitcast_reduce_fusion.1
  589.1 3.0 bitcast_reduce_fusion
  592.8 1.3 convolution_bitcast_fusion.4
  597.0 1.6 fusion.1
  598.7 33.4 %collective-permute-done.15 = bf16[2,2048,256]{1,2,0:T(8,128)(2,1)S(1)} collective-permute-done((bf16[2,2048,256]{1,2,0:T(8,128)(2,1)S(1)}, bf16[2,2048,256]{1,2,0:T(8,128)(2,1)S(1)}, u32[]{:S(2)}, u32[]{:S(2)}) %collective-permute-start.15) | collective-permute-done | bytes 2097184 | tf_op jit(solution)/shard_map/ppermute | solution.py:15
  (115 shorter events, 22.8 us)
Async XLA Ops:
  6.5 430.9 %copy-start = (bf16[2560,2,256]{2,1,0:T(2,128)(2,1)S(1)}, bf16[2560,2,256]{2,1,0:T(2,128)(2,1)}, u32[]{:S(2)}) copy-start(bf16[2560,2,256]{2,1,0:T(2,128)(2,1)} %param.13) | copy-start | bytes 7864324
  6.5 118.0 %copy-start.12 = (bf16[512,64]{0,1:T(8,128)(2,1)S(1)}, bf16[512,64]{0,1:T(8,128)(2,1)}, u32[]{:S(2)}) copy-start(bf16[512,64]{0,1:T(8,128)(2,1)} %param.10) | copy-start | bytes 196612
  6.5 118.0 %copy-start.13 = (bf16[64,320]{1,0:T(8,128)(2,1)S(1)}, bf16[64,320]{1,0:T(8,128)(2,1)}, u32[]{:S(2)}) copy-start(bf16[64,320]{1,0:T(8,128)(2,1)} %param.12) | copy-start | bytes 122884
  6.5 118.0 %all-reduce.3.cloned.1.call-start = ((), (), s32[]{:S(2)}) async-start(), calls=%async_computation | async-start | bytes 131072 | tf_op jit(solution)/shard_map/psum | solution.py:30
  9.2 20.8 %collective-permute-start.1 = (bf16[8]{0:T(256)(128)(2,1)S(1)}, bf16[8]{0:T(256)(128)(2,1)S(1)}, u32[]{:S(2)}, u32[]{:S(2)}) collective-permute-start(bf16[8]{0:T(256)(128)(2,1)S(1)} %get-tuple-element.18), channel_id=1, source_target_pairs={{0,1},{1,0},{2,3},{3,2},{4,5},{5,4},{6,7},{7,6},{8,9},{9,8},{10,11... | collective-permute-start | bytes 56 | tf_op jit(solution)/shard_map/ppermute | solution.py:15
  21.0 434.2 %copy-start.3 = (bf16[2,256,256]{1,2,0:T(8,128)(2,1)}, bf16[2,256,256]{1,2,0:T(8,128)(2,1)S(1)}, u32[]{:S(2)}) copy-start(bf16[2,256,256]{1,2,0:T(8,128)(2,1)S(1)} %copy.207) | copy-start | bytes 786436
  21.0 434.2 %collective-permute-start.2 = (bf16[2,256,256]{1,2,0:T(8,128)(2,1)S(1)}, bf16[2,256,256]{1,2,0:T(8,128)(2,1)S(1)}, u32[]{:S(2)}, u32[]{:S(2)}) collective-permute-start(bf16[2,256,256]{1,2,0:T(8,128)(2,1)S(1)} %copy.207), channel_id=1, source_target_pairs={{0,1},{1,0},{2,3},{3,2},{4,5},{5,4},{6,7},{7,6},{8,9},{9,8},{10,11... | collective-permute-start | bytes 786440 | tf_op jit(solution)/shard_map/ppermute | solution.py:15
  24.7 464.2 %collective-permute-start.3 = (bf16[2,256,256]{1,2,0:T(8,128)(2,1)}, bf16[2,256,256]{1,2,0:T(8,128)(2,1)}, u32[]{:S(2)}, u32[]{:S(2)}) collective-permute-start(bf16[2,256,256]{1,2,0:T(8,128)(2,1)} %copy.212), channel_id=1, source_target_pairs={{0,1},{1,0},{2,3},{3,2},{4,5},{5,4},{6,7},{7,6},{8,9},{9,8},{10,11... | collective-permute-start | bytes 786440 | tf_op jit(solution)/shard_map/ppermute | solution.py:15
  30.1 4.3 collective-permute-start.5
  34.5 5.2 collective-permute-start.9
  39.7 4.3 collective-permute-start.13
  126.6 325.9 %copy-start.1 = (bf16[2,256,256]{2,1,0:T(8,128)(2,1)S(1)}, bf16[2,256,256]{2,1,0:T(8,128)(2,1)}, u32[]{:S(2)}) copy-start(bf16[2,256,256]{2,1,0:T(8,128)(2,1)} %param.15) | copy-start | bytes 786436
  126.6 325.9 %copy-start.23 = (f32[8]{0:T(128)S(1)}, f32[8]{0:T(128)}, u32[]{:S(2)}) copy-start(f32[8]{0:T(128)} %get-tuple-element.17) | copy-start | bytes 100
  437.4 22.7 %copy-start.25 = (f32[8]{0:T(128)S(1)}, f32[8]{0:T(128)}, u32[]{:S(2)}) copy-start(f32[8]{0:T(128)} %convert_element_type.88) | copy-start | bytes 100
  437.9 15.3 %collective-permute-start = (bf16[8,2,256]{2,0,1:T(8,128)(2,1)S(1)}, bf16[8,2,256]{2,0,1:T(8,128)(2,1)S(1)}, u32[]{:S(2)}, u32[]{:S(2)}) collective-permute-start(bf16[8,2,256]{2,0,1:T(8,128)(2,1)S(1)} %fusion.50), channel_id=1, source_target_pairs={{0,1},{1,0},{2,3},{3,2},{4,5},{5,4},{6,7},{7,6},{8,9},{9,8},{10,11... | collective-permute-start | bytes 24584 | tf_op jit(solution)/shard_map/ppermute | solution.py:15
  453.2 7.6 %collective-permute-start.4 = (bf16[16,2,256]{2,0,1:T(8,128)(2,1)S(1)}, bf16[16,2,256]{2,0,1:T(8,128)(2,1)S(1)}, u32[]{:S(2)}, u32[]{:S(2)}) collective-permute-start(bf16[16,2,256]{2,0,1:T(8,128)(2,1)S(1)} %pad_maximum_fusion.8), channel_id=1, source_target_pairs={{0,2},{1,3},{2,0},{3,1},{4,6},{5,7},{6,4},{7,5},{8,10},{9,11},{10,... | collective-permute-start | bytes 49160 | tf_op jit(solution)/shard_map/ppermute | solution.py:15
  455.2 0.7 copy-start.4
  456.7 15.9 %collective-permute-start.6 = (bf16[2,512,256]{1,2,0:T(8,128)(2,1)}, bf16[2,512,256]{1,2,0:T(8,128)(2,1)S(1)}, u32[]{:S(2)}, u32[]{:S(2)}) collective-permute-start(bf16[2,512,256]{1,2,0:T(8,128)(2,1)} %pad_maximum_fusion.4), channel_id=1, source_target_pairs={{0,2},{1,3},{2,0},{3,1},{4,6},{5,7},{6,4},{7,5},{8,10},{9,11},{10,... | collective-permute-start | bytes 1572872 | tf_op jit(solution)/shard_map/ppermute | solution.py:15
  460.9 2.5 copy-start.9
  461.5 18.0 %collective-permute-start.8 = (bf16[32,2,256]{2,0,1:T(8,128)(2,1)}, bf16[32,2,256]{2,0,1:T(8,128)(2,1)}, u32[]{:S(2)}, u32[]{:S(2)}) collective-permute-start(bf16[32,2,256]{2,0,1:T(8,128)(2,1)} %pad_maximum_fusion.7), channel_id=1, source_target_pairs={{0,4},{1,5},{2,6},{3,7},{4,0},{5,1},{6,2},{7,3},{8,12},{9,13},{10,... | collective-permute-start | bytes 98312 | tf_op jit(solution)/shard_map/ppermute | solution.py:15
  464.6 12.1 %copy-start.19 = (bf16[16,2,128]{2,1,0:T(2,128)(2,1)S(1)}, bf16[16,2,128]{2,1,0:T(2,128)(2,1)}, u32[]{:S(2)}) copy-start(bf16[16,2,128]{2,1,0:T(2,128)(2,1)} %reshape_squeeze.34) | copy-start | bytes 24580
  474.8 50.5 %collective-permute-start.10 = (bf16[2,1024,256]{1,2,0:T(8,128)(2,1)}, bf16[2,1024,256]{1,2,0:T(8,128)(2,1)}, u32[]{:S(2)}, u32[]{:S(2)}) collective-permute-start(bf16[2,1024,256]{1,2,0:T(8,128)(2,1)} %pad_maximum_fusion.2), channel_id=1, source_target_pairs={{0,4},{1,5},{2,6},{3,7},{4,0},{5,1},{6,2},{7,3},{8,12},{9,13},{10,... | collective-permute-start | bytes 3145736 | tf_op jit(solution)/shard_map/ppermute | solution.py:15
  480.9 12.3 %collective-permute-start.12 = (bf16[64,2,256]{2,0,1:T(8,128)(2,1)}, bf16[64,2,256]{2,0,1:T(8,128)(2,1)}, u32[]{:S(2)}, u32[]{:S(2)}) collective-permute-start(bf16[64,2,256]{2,0,1:T(8,128)(2,1)} %pad_maximum_fusion.6), channel_id=1, source_target_pairs={{0,8},{1,9},{2,10},{3,11},{4,12},{5,13},{6,14},{7,15},{8,0},{9,1},... | collective-permute-start | bytes 196616 | tf_op jit(solution)/shard_map/ppermute | solution.py:15
  490.8 42.3 %collective-permute-start.7 = (bf16[2,512,256]{1,2,0:T(8,128)(2,1)}, bf16[2,512,256]{1,2,0:T(8,128)(2,1)}, u32[]{:S(2)}, u32[]{:S(2)}) collective-permute-start(bf16[2,512,256]{1,2,0:T(8,128)(2,1)} %pad_maximum_fusion.5), channel_id=1, source_target_pairs={{0,2},{1,3},{2,0},{3,1},{4,6},{5,7},{6,4},{7,5},{8,10},{9,11},{10,... | collective-permute-start | bytes 1572872 | tf_op jit(solution)/shard_map/ppermute | solution.py:15
  496.0 34.2 %copy-start.10 = (bf16[64,2,128]{2,1,0:T(2,128)(2,1)S(1)}, bf16[64,2,128]{2,1,0:T(2,128)(2,1)}, u32[]{:S(2)}) copy-start(bf16[64,2,128]{2,1,0:T(2,128)(2,1)} %reshape_squeeze.38) | copy-start | bytes 98308
  496.0 34.2 %copy-start.24 = (f32[64]{0:T(128)S(1)}, f32[64]{0:T(128)}, u32[]{:S(2)}) copy-start(f32[64]{0:T(128)} %convert_element_type.97) | copy-start | bytes 772
  528.3 60.8 %collective-permute-start.14 = (bf16[2,2048,256]{1,2,0:T(8,128)(2,1)}, bf16[2,2048,256]{1,2,0:T(8,128)(2,1)}, u32[]{:S(2)}, u32[]{:S(2)}) collective-permute-start(bf16[2,2048,256]{1,2,0:T(8,128)(2,1)} %pad_maximum_fusion), channel_id=1, source_target_pairs={{0,8},{1,9},{2,10},{3,11},{4,12},{5,13},{6,14},{7,15},{8,0},{9,1},... | collective-permute-start | bytes 6291464 | tf_op jit(solution)/shard_map/ppermute | solution.py:15
  533.1 3.3 copy-start.5
  534.5 47.7 %collective-permute-start.11 = (bf16[2,1024,256]{1,2,0:T(8,128)(2,1)S(1)}, bf16[2,1024,256]{1,2,0:T(8,128)(2,1)S(1)}, u32[]{:S(2)}, u32[]{:S(2)}) collective-permute-start(bf16[2,1024,256]{1,2,0:T(8,128)(2,1)S(1)} %pad_maximum_fusion.3), channel_id=1, source_target_pairs={{0,4},{1,5},{2,6},{3,7},{4,0},{5,1},{6,2},{7,3},{8,12},{9,13},{10,... | collective-permute-start | bytes 3145736 | tf_op jit(solution)/shard_map/ppermute | solution.py:15
  536.4 0.9 copy-start.15
  536.4 0.9 copy-start.17
  536.4 0.9 copy-start.20
  536.4 0.9 copy-start.21
  536.4 1.2 copy-start.2
  536.8 1.0 copy-start.7
  583.5 48.6 %collective-permute-start.15 = (bf16[2,2048,256]{1,2,0:T(8,128)(2,1)S(1)}, bf16[2,2048,256]{1,2,0:T(8,128)(2,1)S(1)}, u32[]{:S(2)}, u32[]{:S(2)}) collective-permute-start(bf16[2,2048,256]{1,2,0:T(8,128)(2,1)S(1)} %pad_maximum_fusion.1), channel_id=1, source_target_pairs={{0,8},{1,9},{2,10},{3,11},{4,12},{5,13},{6,14},{7,15},{8,0},{9,1},... | collective-permute-start | bytes 6291464 | tf_op jit(solution)/shard_map/ppermute | solution.py:15
  589.1 3.0 copy-start.14
  589.1 3.0 copy-start.16
  589.1 3.0 copy-start.6
  589.1 3.1 copy-start.8
  592.3 1.8 copy-start.18
  632.1 0.8 copy-start.11
  632.9 0.9 copy-start.22
Sparse Core Ops, SparseCore 0:
  20.0 104.4 all-reduce.2
where the time goes:
time: 644 us; the launch traced here: 642 us
  blocking collectives  310 us (48%)
  waiting for transfers between devices  201 us (31%)
  starting transfers between devices  54 us (8%)
  matrix products  25.1 us (4%)
  other arithmetic  21.1 us (3%)
  local copies, waits for them, and re-layouts  16.3 us (3%)
  between operations  14.1 us (2%)
    psum x1, blocking collectives, local(): caption_whole = lax.psum(caption_term, 'seq')  272 us
    ppermute x16, waiting for transfers between devices, partner(): return lax.ppermute(value, axis, pairs)  121 us
    psum x1, waiting for transfers between devices, local(): lax.psum(llama_term.astype(jnp.bfloat16), 'tp').astype(jnp.float32)  79.9 us
    ppermute x16, starting transfers between devices, partner(): return lax.ppermute(value, axis, pairs)  54 us
    all_gather x1, blocking collectives, local(): lax.all_gather(text_part.astype(jnp.bfloat16), 'tp', axis=1, tiled=True)  37.7 us
  transfers between devices with their start and end apart: 17, of which 8 were waited for; matrix products, arithmetic and copies ran while one was open for 9% of the time, Pallas kernels for 0%

commit v1 on v0

--- a/solution.py
+++ b/solution.py
@@ -36,7 +36,9 @@
     caption_term = jnp.dot(llama_hidden, w_caption, preferred_element_type=jnp.float32)
     caption_whole = lax.psum(caption_term, "seq")
     text_part = lax.dynamic_slice_in_dim(caption_whole, seq_index * text_rows, text_rows, 0)
-    text_states = lax.all_gather(text_part.astype(jnp.bfloat16), "tp", axis=1, tiled=True)
+    own = text_part.astype(jnp.bfloat16)
+    repeated = jnp.stack([own] * lax.axis_size("tp"))
+    text_states = jnp.concatenate(lax.all_to_all(repeated, "tp", 0, 0), axis=1)
     text_kv = jnp.einsum(
         "td,djc->tjc", text_states, w_text_kv, preferred_element_type=jnp.float32
     ).astype(jnp.bfloat16)

time: 644 us -> 615 us (0.955)
  blocking collectives: 310 us -> 272 us
  waiting for transfers between devices: 201 us -> 211 us
    all_gather x1 -> x0, blocking collectives: 37.7 us -> none  [local(): lax.all_gather(text_part.astype(jnp.bfloat16), 'tp', axis=1, tiled=True)]
    psum x1, waiting for transfers between devices: 79.9 us -> 88.2 us  [local(): lax.psum(llama_term.astype(jnp.bfloat16), 'tp').astype(jnp.float32)]
  transfers between devices with their start and end apart: 17 -> 18, of which waited for: 8 -> 8; matrix products, arithmetic and copies ran while one was open for 9% -> 9% of each run, Pallas kernels for 0% -> 0%
where the time goes in v1:
time: 615 us; the launch traced here: 613 us
  blocking collectives  272 us (44%)
  waiting for transfers between devices  211 us (34%)
  starting transfers between devices  52.3 us (9%)
  matrix products  25.7 us (4%)
  other arithmetic  21.1 us (3%)
  local copies, waits for them, and re-layouts  17 us (3%)
  between operations  14.1 us (2%)
    psum x1, blocking collectives, local(): caption_whole = lax.psum(caption_term, 'seq')  272 us
    ppermute x16, waiting for transfers between devices, partner(): return lax.ppermute(value, axis, pairs)  118 us
    psum x1, waiting for transfers between devices, local(): lax.psum(llama_term.astype(jnp.bfloat16), 'tp').astype(jnp.float32)  88.2 us
    ppermute x16, starting transfers between devices, partner(): return lax.ppermute(value, axis, pairs)  49 us
  transfers between devices with their start and end apart: 18, of which 8 were waited for; matrix products, arithmetic and copies ran while one was open for 9% of the time, Pallas kernels for 0%

profile of v1, /device:TPU:1, one launch (start us, length us, event | category | flops | bytes accessed | tf_op | source)
XLA Modules:
  0.0 613.1 jit_solution(5446837464490521098)
XLA Ops:
  6.6 1.4 fusion.126
  9.2 8.7 %collective-permute-start.1 = (bf16[8]{0:T(256)(128)(2,1)S(1)}, bf16[8]{0:T(256)(128)(2,1)S(1)}, u32[]{:S(2)}, u32[]{:S(2)}) collective-permute-start(bf16[8]{0:T(256)(128)(2,1)S(1)} %get-tuple-element.18), channel_id=1, source_target_pairs={{0,1},{1,0},{2,3},{3,2},{4,5},{5,4},{6,7},{7,6},{8,9},{9,8},{10,11... | collective-permute-start | bytes 56 | tf_op jit(solution)/shard_map/ppermute | solution.py:15
  17.9 2.0 convolution_convert_fusion
  21.0 1.9 collective-permute-start.2
  23.0 1.8 copy.211
  24.7 2.4 collective-permute-start.3
  27.1 2.9 fusion.149
  30.1 1.9 collective-permute-start.5
  32.6 1.8 collective-permute-done.5
  34.5 1.9 collective-permute-start.9
  36.4 88.2 %all-reduce.3.cloned.1.call-done = bf16[512,64]{0,1:T(8,128)(2,1)} async-done(((bf16[512,64]{0,1:T(8,128)(2,1)}), bf16[512,64]{0,1:T(8,128)(2,1)}) %all-reduce.3.cloned.1.call-update) | async-done | bytes 65552 | tf_op jit(solution)/shard_map/psum | solution.py:30
  124.6 2.0 fusion.97
  126.6 272.4 %all-reduce.4 = bf16[512,320]{1,0:T(8,128)(2,1)} all-reduce(f32[512,320]{1,0:T(8,128)} %fusion.97), channel_id=1, replica_groups=mesh['tp'=8,'seq'=64] {'seq'}, use_global_device_ids=true, to_apply=%region_1.0 | all-reduce | flops 163840 | bytes 983040 | tf_op jit(solution)/shard_map/psum | solution.py:37
  400.3 3.3 all-to-all-start
  403.8 1.9 collective-permute-start.13
  408.6 4.1 all-to-all-done
  413.2 9.5 %collective-permute-start = (bf16[8,2,256]{2,0,1:T(8,128)(2,1)S(1)}, bf16[8,2,256]{2,0,1:T(8,128)(2,1)S(1)}, u32[]{:S(2)}, u32[]{:S(2)}) collective-permute-start(bf16[8,2,256]{2,0,1:T(8,128)(2,1)S(1)} %fusion.50), channel_id=1, source_target_pairs={{0,1},{1,0},{2,3},{3,2},{4,5},{5,4},{6,7},{7,6},{8,9},{9,8},{10,11... | collective-permute-start | bytes 24584 | tf_op jit(solution)/shard_map/ppermute | solution.py:15
  422.7 1.4 fusion.148
  424.1 1.9 collective-permute-start.4
  427.6 3.3 collective-permute-start.6
  432.4 1.9 collective-permute-start.8
  435.5 8.3 %collective-permute-done.6 = bf16[2,512,256]{1,2,0:T(8,128)(2,1)S(1)} collective-permute-done((bf16[2,512,256]{1,2,0:T(8,128)(2,1)}, bf16[2,512,256]{1,2,0:T(8,128)(2,1)S(1)}, u32[]{:S(2)}, u32[]{:S(2)}) %collective-permute-start.6) | collective-permute-done | bytes 524320 | tf_op jit(solution)/shard_map/ppermute | solution.py:15
  443.9 2.2 pad_maximum_fusion.2
  446.0 1.9 collective-permute-start.10
  448.0 1.4 fusion.145
  450.7 1.4 pad_maximum_fusion.6
  452.1 1.9 collective-permute-start.12
  454.0 1.4 fusion.141
  458.0 2.2 fusion.144
  460.2 1.9 pad_maximum_fusion.5
  462.0 2.4 collective-permute-start.7
  464.4 1.4 fusion.140
  465.8 1.4 reshape_squeeze.38
  467.2 29.3 %collective-permute-done.10 = bf16[2,1024,256]{1,2,0:T(8,128)(2,1)} collective-permute-done((bf16[2,1024,256]{1,2,0:T(8,128)(2,1)}, bf16[2,1024,256]{1,2,0:T(8,128)(2,1)}, u32[]{:S(2)}, u32[]{:S(2)}) %collective-permute-start.10) | collective-permute-done | bytes 1048608 | tf_op jit(solution)/shard_map/ppermute | solution.py:15
  496.6 3.0 pad_maximum_fusion
  499.5 1.9 collective-permute-start.14
  501.5 1.5 fusion.143
  503.0 1.4 reshape_squeeze.39
  504.4 1.3 pad_maximum_fusion.3
  505.7 1.9 collective-permute-start.11
  509.4 44.0 %collective-permute-done.11 = bf16[2,1024,256]{1,2,0:T(8,128)(2,1)S(1)} collective-permute-done((bf16[2,1024,256]{1,2,0:T(8,128)(2,1)S(1)}, bf16[2,1024,256]{1,2,0:T(8,128)(2,1)S(1)}, u32[]{:S(2)}, u32[]{:S(2)}) %collective-permute-start.11) | collective-permute-done | bytes 1048608 | tf_op jit(solution)/shard_map/ppermute | solution.py:15
  553.4 1.4 pad_maximum_fusion.1
  554.8 3.5 collective-permute-start.15
  558.3 2.0 bitcast_reduce_fusion.1
  560.4 3.0 bitcast_reduce_fusion
  564.0 1.3 convolution_bitcast_fusion.4
  568.3 1.6 fusion.1
  569.9 33.4 %collective-permute-done.15 = bf16[2,2048,256]{1,2,0:T(8,128)(2,1)S(1)} collective-permute-done((bf16[2,2048,256]{1,2,0:T(8,128)(2,1)S(1)}, bf16[2,2048,256]{1,2,0:T(8,128)(2,1)S(1)}, u32[]{:S(2)}, u32[]{:S(2)}) %collective-permute-start.15) | collective-permute-done | bytes 2097184 | tf_op jit(solution)/shard_map/ppermute | solution.py:15
  (115 shorter events, 24.0 us)
Async XLA Ops:
  6.5 406.2 %copy-start = (bf16[2560,2,256]{2,1,0:T(2,128)(2,1)S(1)}, bf16[2560,2,256]{2,1,0:T(2,128)(2,1)}, u32[]{:S(2)}) copy-start(bf16[2560,2,256]{2,1,0:T(2,128)(2,1)} %param.13) | copy-start | bytes 7864324
  6.5 118.1 %copy-start.12 = (bf16[512,64]{0,1:T(8,128)(2,1)S(1)}, bf16[512,64]{0,1:T(8,128)(2,1)}, u32[]{:S(2)}) copy-start(bf16[512,64]{0,1:T(8,128)(2,1)} %param.10) | copy-start | bytes 196612
  6.5 118.1 %copy-start.13 = (bf16[64,320]{1,0:T(8,128)(2,1)S(1)}, bf16[64,320]{1,0:T(8,128)(2,1)}, u32[]{:S(2)}) copy-start(bf16[64,320]{1,0:T(8,128)(2,1)} %param.12) | copy-start | bytes 122884
  6.5 118.1 %all-reduce.3.cloned.1.call-start = ((), (), s32[]{:S(2)}) async-start(), calls=%async_computation.1 | async-start | bytes 131072 | tf_op jit(solution)/shard_map/psum | solution.py:30
  9.2 20.8 %collective-permute-start.1 = (bf16[8]{0:T(256)(128)(2,1)S(1)}, bf16[8]{0:T(256)(128)(2,1)S(1)}, u32[]{:S(2)}, u32[]{:S(2)}) collective-permute-start(bf16[8]{0:T(256)(128)(2,1)S(1)} %get-tuple-element.18), channel_id=1, source_target_pairs={{0,1},{1,0},{2,3},{3,2},{4,5},{5,4},{6,7},{7,6},{8,9},{9,8},{10,11... | collective-permute-start | bytes 56 | tf_op jit(solution)/shard_map/ppermute | solution.py:15
  21.0 405.1 %copy-start.3 = (bf16[2,256,256]{1,2,0:T(8,128)(2,1)}, bf16[2,256,256]{1,2,0:T(8,128)(2,1)S(1)}, u32[]{:S(2)}) copy-start(bf16[2,256,256]{1,2,0:T(8,128)(2,1)S(1)} %copy.206) | copy-start | bytes 786436
  21.0 405.0 %collective-permute-start.2 = (bf16[2,256,256]{1,2,0:T(8,128)(2,1)S(1)}, bf16[2,256,256]{1,2,0:T(8,128)(2,1)S(1)}, u32[]{:S(2)}, u32[]{:S(2)}) collective-permute-start(bf16[2,256,256]{1,2,0:T(8,128)(2,1)S(1)} %copy.206), channel_id=1, source_target_pairs={{0,1},{1,0},{2,3},{3,2},{4,5},{5,4},{6,7},{7,6},{8,9},{9,8},{10,11... | collective-permute-start | bytes 786440 | tf_op jit(solution)/shard_map/ppermute | solution.py:15
  24.7 435.4 %collective-permute-start.3 = (bf16[2,256,256]{1,2,0:T(8,128)(2,1)}, bf16[2,256,256]{1,2,0:T(8,128)(2,1)}, u32[]{:S(2)}, u32[]{:S(2)}) collective-permute-start(bf16[2,256,256]{1,2,0:T(8,128)(2,1)} %copy.211), channel_id=1, source_target_pairs={{0,1},{1,0},{2,3},{3,2},{4,5},{5,4},{6,7},{7,6},{8,9},{9,8},{10,11... | collective-permute-start | bytes 786440 | tf_op jit(solution)/shard_map/ppermute | solution.py:15
  30.1 4.3 collective-permute-start.5
  34.5 369.2 %collective-permute-start.9 = (bf16[32]{0:T(256)(128)(2,1)S(1)}, bf16[32]{0:T(256)(128)(2,1)S(1)}, u32[]{:S(2)}, u32[]{:S(2)}) collective-permute-start(bf16[32]{0:T(256)(128)(2,1)S(1)} %pad_maximum_fusion.10), channel_id=1, source_target_pairs={{0,4},{1,5},{2,6},{3,7},{4,0},{5,1},{6,2},{7,3},{8,12},{9,13},{10,... | collective-permute-start | bytes 200 | tf_op jit(solution)/shard_map/ppermute | solution.py:15
  126.6 296.1 %copy-start.1 = (bf16[2,256,256]{2,1,0:T(8,128)(2,1)S(1)}, bf16[2,256,256]{2,1,0:T(8,128)(2,1)}, u32[]{:S(2)}) copy-start(bf16[2,256,256]{2,1,0:T(8,128)(2,1)} %param.15) | copy-start | bytes 786436
  400.3 12.3 %all-to-all-start = ((bf16[8,8,320]{2,1,0:T(8,128)(2,1)}), bf16[8,8,320]{2,1,0:T(8,128)(2,1)S(1)}, u32[]{:S(2)}, u32[]{:S(2)}) async-start(bf16[8,8,320]{2,1,0:T(8,128)(2,1)} %stack.2), calls=%async_computation | async-start | bytes 98304 | tf_op jit(solution)/shard_map/all_to_all | solution.py:41
  403.8 4.3 collective-permute-start.13
  412.8 18.2 %copy-start.24 = (f32[8]{0:T(128)S(1)}, f32[8]{0:T(128)}, u32[]{:S(2)}) copy-start(f32[8]{0:T(128)} %convert_element_type.88) | copy-start | bytes 100
  413.2 10.9 %collective-permute-start = (bf16[8,2,256]{2,0,1:T(8,128)(2,1)S(1)}, bf16[8,2,256]{2,0,1:T(8,128)(2,1)S(1)}, u32[]{:S(2)}, u32[]{:S(2)}) collective-permute-start(bf16[8,2,256]{2,0,1:T(8,128)(2,1)S(1)} %fusion.50), channel_id=1, source_target_pairs={{0,1},{1,0},{2,3},{3,2},{4,5},{5,4},{6,7},{7,6},{8,9},{9,8},{10,11... | collective-permute-start | bytes 24584 | tf_op jit(solution)/shard_map/ppermute | solution.py:15
  424.1 7.6 %collective-permute-start.4 = (bf16[16,2,256]{2,0,1:T(8,128)(2,1)S(1)}, bf16[16,2,256]{2,0,1:T(8,128)(2,1)S(1)}, u32[]{:S(2)}, u32[]{:S(2)}) collective-permute-start(bf16[16,2,256]{2,0,1:T(8,128)(2,1)S(1)} %pad_maximum_fusion.8), channel_id=1, source_target_pairs={{0,2},{1,3},{2,0},{3,1},{4,6},{5,7},{6,4},{7,5},{8,10},{9,11},{10,... | collective-permute-start | bytes 49160 | tf_op jit(solution)/shard_map/ppermute | solution.py:15
  426.1 0.7 copy-start.4
  427.6 16.3 %collective-permute-start.6 = (bf16[2,512,256]{1,2,0:T(8,128)(2,1)}, bf16[2,512,256]{1,2,0:T(8,128)(2,1)S(1)}, u32[]{:S(2)}, u32[]{:S(2)}) collective-permute-start(bf16[2,512,256]{1,2,0:T(8,128)(2,1)} %pad_maximum_fusion.4), channel_id=1, source_target_pairs={{0,2},{1,3},{2,0},{3,1},{4,6},{5,7},{6,4},{7,5},{8,10},{9,11},{10,... | collective-permute-start | bytes 1572872 | tf_op jit(solution)/shard_map/ppermute | solution.py:15
  431.8 2.5 copy-start.9
  432.4 18.3 %collective-permute-start.8 = (bf16[32,2,256]{2,0,1:T(8,128)(2,1)}, bf16[32,2,256]{2,0,1:T(8,128)(2,1)}, u32[]{:S(2)}, u32[]{:S(2)}) collective-permute-start(bf16[32,2,256]{2,0,1:T(8,128)(2,1)} %pad_maximum_fusion.7), channel_id=1, source_target_pairs={{0,4},{1,5},{2,6},{3,7},{4,0},{5,1},{6,2},{7,3},{8,12},{9,13},{10,... | collective-permute-start | bytes 98312 | tf_op jit(solution)/shard_map/ppermute | solution.py:15
  435.5 12.4 %copy-start.19 = (bf16[16,2,128]{2,1,0:T(2,128)(2,1)S(1)}, bf16[16,2,128]{2,1,0:T(2,128)(2,1)}, u32[]{:S(2)}) copy-start(bf16[16,2,128]{2,1,0:T(2,128)(2,1)} %reshape_squeeze.34) | copy-start | bytes 24580
  446.0 50.5 %collective-permute-start.10 = (bf16[2,1024,256]{1,2,0:T(8,128)(2,1)}, bf16[2,1024,256]{1,2,0:T(8,128)(2,1)}, u32[]{:S(2)}, u32[]{:S(2)}) collective-permute-start(bf16[2,1024,256]{1,2,0:T(8,128)(2,1)} %pad_maximum_fusion.2), channel_id=1, source_target_pairs={{0,4},{1,5},{2,6},{3,7},{4,0},{5,1},{6,2},{7,3},{8,12},{9,13},{10,... | collective-permute-start | bytes 3145736 | tf_op jit(solution)/shard_map/ppermute | solution.py:15
  452.1 12.4 %collective-permute-start.12 = (bf16[64,2,256]{2,0,1:T(8,128)(2,1)}, bf16[64,2,256]{2,0,1:T(8,128)(2,1)}, u32[]{:S(2)}, u32[]{:S(2)}) collective-permute-start(bf16[64,2,256]{2,0,1:T(8,128)(2,1)} %pad_maximum_fusion.6), channel_id=1, source_target_pairs={{0,8},{1,9},{2,10},{3,11},{4,12},{5,13},{6,14},{7,15},{8,0},{9,1},... | collective-permute-start | bytes 196616 | tf_op jit(solution)/shard_map/ppermute | solution.py:15
  462.0 42.3 %collective-permute-start.7 = (bf16[2,512,256]{1,2,0:T(8,128)(2,1)}, bf16[2,512,256]{1,2,0:T(8,128)(2,1)}, u32[]{:S(2)}, u32[]{:S(2)}) collective-permute-start(bf16[2,512,256]{1,2,0:T(8,128)(2,1)} %pad_maximum_fusion.5), channel_id=1, source_target_pairs={{0,2},{1,3},{2,0},{3,1},{4,6},{5,7},{6,4},{7,5},{8,10},{9,11},{10,... | collective-permute-start | bytes 1572872 | tf_op jit(solution)/shard_map/ppermute | solution.py:15
  467.2 34.2 %copy-start.10 = (bf16[64,2,128]{2,1,0:T(2,128)(2,1)S(1)}, bf16[64,2,128]{2,1,0:T(2,128)(2,1)}, u32[]{:S(2)}) copy-start(bf16[64,2,128]{2,1,0:T(2,128)(2,1)} %reshape_squeeze.38) | copy-start | bytes 98308
  467.2 34.2 %copy-start.23 = (f32[64]{0:T(128)S(1)}, f32[64]{0:T(128)}, u32[]{:S(2)}) copy-start(f32[64]{0:T(128)} %convert_element_type.97) | copy-start | bytes 772
  499.5 60.8 %collective-permute-start.14 = (bf16[2,2048,256]{1,2,0:T(8,128)(2,1)}, bf16[2,2048,256]{1,2,0:T(8,128)(2,1)}, u32[]{:S(2)}, u32[]{:S(2)}) collective-permute-start(bf16[2,2048,256]{1,2,0:T(8,128)(2,1)} %pad_maximum_fusion), channel_id=1, source_target_pairs={{0,8},{1,9},{2,10},{3,11},{4,12},{5,13},{6,14},{7,15},{8,0},{9,1},... | collective-permute-start | bytes 6291464 | tf_op jit(solution)/shard_map/ppermute | solution.py:15
  504.3 3.3 copy-start.5
  505.7 47.7 %collective-permute-start.11 = (bf16[2,1024,256]{1,2,0:T(8,128)(2,1)S(1)}, bf16[2,1024,256]{1,2,0:T(8,128)(2,1)S(1)}, u32[]{:S(2)}, u32[]{:S(2)}) collective-permute-start(bf16[2,1024,256]{1,2,0:T(8,128)(2,1)S(1)} %pad_maximum_fusion.3), channel_id=1, source_target_pairs={{0,4},{1,5},{2,6},{3,7},{4,0},{5,1},{6,2},{7,3},{8,12},{9,13},{10,... | collective-permute-start | bytes 3145736 | tf_op jit(solution)/shard_map/ppermute | solution.py:15
  507.6 0.9 copy-start.15
  507.6 0.9 copy-start.17
  507.7 0.9 copy-start.20
  507.7 0.9 copy-start.21
  507.7 1.2 copy-start.2
  508.0 1.0 copy-start.7
  554.8 48.6 %collective-permute-start.15 = (bf16[2,2048,256]{1,2,0:T(8,128)(2,1)S(1)}, bf16[2,2048,256]{1,2,0:T(8,128)(2,1)S(1)}, u32[]{:S(2)}, u32[]{:S(2)}) collective-permute-start(bf16[2,2048,256]{1,2,0:T(8,128)(2,1)S(1)} %pad_maximum_fusion.1), channel_id=1, source_target_pairs={{0,8},{1,9},{2,10},{3,11},{4,12},{5,13},{6,14},{7,15},{8,0},{9,1},... | collective-permute-start | bytes 6291464 | tf_op jit(solution)/shard_map/ppermute | solution.py:15
  560.3 3.0 copy-start.14
  560.3 3.0 copy-start.16
  560.3 3.0 copy-start.6
  560.4 3.1 copy-start.8
  563.6 1.8 copy-start.18
  603.4 0.8 copy-start.11
  604.1 0.9 copy-start.22
Sparse Core Ops, SparseCore 0:
  20.0 104.5 all-reduce.2
